TPU v7x, 32 devices: a whole 2x2x4 slice. The times are simulated.
32 devices in a mesh: row: 8 (over z, x), col: 4 (over y, core).
Axes of the slice: x: 2, y: 2, z: 4, core: 2. Of those that a mesh axis runs over, the one named last changes fastest.
Arguments:
- alignment: bfloat16 [256, 192, 256], P('row', 'col'), may hold values from -8 to 8
- alignment_mask: int32 [256, 192], P('row', 'col'), may hold values from 0 to 1, as said below
- residue_mask: int32 [192], replicated, may hold values from 0 to 1, as said below
- pair_features: bfloat16 [192, 192, 128], P('row', 'col'), may hold values from -6 to 6
- outer_product_left: bfloat16 [256, 32], replicated, may hold values from -0.375 to 0.375
- outer_product_right: bfloat16 [256, 32], replicated, may hold values from -0.375 to 0.375
- outer_proj: bfloat16 [1024, 128], replicated, may hold values from -0.1875 to 0.1875
- triangle_proj: bfloat16 [128, 512], replicated, may hold values from -0.5 to 0.5
- triangle_gate: bfloat16 [128, 128], replicated, may hold values from -0.5 to 0.5
- triangle_out: bfloat16 [128, 128], replicated, may hold values from -0.5 to 0.5
- transition_in: bfloat16 [128, 512], replicated, may hold values from -0.5 to 0.5
- transition_out: bfloat16 [512, 128], replicated, may hold values from -0.25 to 0.25
Outputs:
- pair_out: bfloat16 [192, 192, 128], P('row', 'col')
Inputs may be any that keep to these rules, and one draw needn't show every extreme that they name: `residue_mask`: masked residues scattered anywhere; at least one residue is masked and at least one takes part. `alignment_mask`: 0 wherever residue_mask is 0.
All inputs are finite; a program needn't handle non-finite values.
Results may differ from a plain program's by a relative error of at most 0.014.
Values may be sent and summed in bfloat16 or wider, within the bound.
No kernel may reach another device: no remote copies, remote signals or barrier semaphores. Data moves between devices by JAX's collectives and lax.ppermute only.
A program may use at most 64 MiB of HBM per device.

v0:
```python
import jax
import jax.numpy as jnp
from jax import lax
from jax.sharding import PartitionSpec as P

epsilon = 1e-05


def normalize(values):
    mean_value = jnp.mean(values, axis=-1, keepdims=True)
    centered = values - mean_value
    variance = jnp.mean(centered * centered, axis=-1, keepdims=True)
    return centered * lax.rsqrt(variance + epsilon)


def shards(
    alignment,
    alignment_mask,
    residue_mask,
    pair_features,
    outer_product_left,
    outer_product_right,
    outer_proj,
    triangle_proj,
    triangle_gate,
    triangle_out,
    transition_in,
    transition_out,
):
    block_rows, block_cols, channels = pair_features.shape
    inner = triangle_out.shape[0]
    narrow = outer_product_left.shape[1]
    mask_float = alignment_mask.astype(jnp.float32)
    normed = normalize(alignment.astype(jnp.float32)).astype(jnp.bfloat16)
    left_side = (
        jnp.dot(normed, outer_product_left, preferred_element_type=jnp.float32)
        * mask_float[..., None]
    ).astype(jnp.bfloat16)
    right_side = (
        jnp.dot(normed, outer_product_right, preferred_element_type=jnp.float32)
        * mask_float[..., None]
    ).astype(jnp.bfloat16)
    mask_wire = alignment_mask.astype(jnp.bfloat16)
    right_all, right_mask = (
        lax.all_gather(right_side, "row", axis=0, tiled=True),
        lax.all_gather(mask_wire, "row", axis=0, tiled=True),
    )
    left_rows, left_row_mask = (
        lax.all_gather(left_side, "col", axis=1, tiled=True),
        lax.all_gather(mask_wire, "col", axis=1, tiled=True),
    )
    left_all, left_mask = (
        lax.all_to_all(left_rows, "row", split_axis=1, concat_axis=0, tiled=True),
        lax.all_to_all(left_row_mask, "row", split_axis=1, concat_axis=0, tiled=True),
    )
    sequences = left_all.shape[0]
    contract = (((0,), (0,)), ((), ()))
    outer = lax.dot_general(
        left_all.reshape(sequences, block_rows * narrow),
        right_all.reshape(sequences, block_cols * narrow),
        contract,
        preferred_element_type=jnp.float32,
    )
    outer = (
        outer.reshape(block_rows, narrow, block_cols, narrow)
        .transpose(0, 2, 1, 3)
        .astype(jnp.bfloat16)
    )
    outer = outer.reshape(block_rows, block_cols, narrow * narrow)
    projected = jnp.dot(outer, outer_proj, preferred_element_type=jnp.float32)
    counts = lax.dot_general(left_mask, right_mask, contract, preferred_element_type=jnp.float32)
    first = (
        pair_features.astype(jnp.float32) + projected / jnp.maximum(counts, 1.0)[..., None]
    ).astype(jnp.bfloat16)
    normed_pair = normalize(first.astype(jnp.float32)).astype(jnp.bfloat16)
    projections = jnp.dot(normed_pair, triangle_proj, preferred_element_type=jnp.float32)
    row_mask = lax.dynamic_slice_in_dim(
        residue_mask, lax.axis_index("row") * block_rows, block_rows
    ).astype(jnp.float32)
    col_mask = lax.dynamic_slice_in_dim(
        residue_mask, lax.axis_index("col") * block_cols, block_cols
    ).astype(jnp.float32)
    pair_mask = (row_mask[:, None] * col_mask[None, :])[..., None]
    left_tri = (
        jax.nn.sigmoid(projections[..., :inner]) * projections[..., inner : 2 * inner] * pair_mask
    ).astype(jnp.bfloat16)
    right_tri = (
        jax.nn.sigmoid(projections[..., 2 * inner : 3 * inner])
        * projections[..., 3 * inner :]
        * pair_mask
    ).astype(jnp.bfloat16)
    right_cols = lax.all_gather(right_tri, "row", axis=0, tiled=True)
    right_rows = lax.all_to_all(right_cols, "col", split_axis=0, concat_axis=1, tiled=True)
    summed = jnp.einsum(
        "ikc,jkc->ijc",
        lax.all_gather(left_tri, "col", axis=1, tiled=True),
        right_rows,
        preferred_element_type=jnp.float32,
    )
    normed_sum = normalize(summed).astype(jnp.bfloat16)
    update = jax.nn.sigmoid(
        jnp.dot(normed_pair, triangle_gate, preferred_element_type=jnp.float32)
    ) * jnp.dot(normed_sum, triangle_out, preferred_element_type=jnp.float32)
    second = (first.astype(jnp.float32) + update).astype(jnp.bfloat16)
    normed_second = normalize(second.astype(jnp.float32)).astype(jnp.bfloat16)
    hidden_units = jnp.maximum(
        jnp.dot(normed_second, transition_in, preferred_element_type=jnp.float32), 0.0
    ).astype(jnp.bfloat16)
    return (
        second.astype(jnp.float32)
        + jnp.dot(hidden_units, transition_out, preferred_element_type=jnp.float32)
    ).astype(jnp.bfloat16)


def solution(mesh):
    placed = (
        P("row", "col", None),
        P("row", "col"),
        P(),
        P("row", "col", None),
        P(),
        P(),
        P(),
        P(),
        P(),
        P(),
        P(),
        P(),
    )
    return jax.shard_map(
        shards, mesh=mesh, in_specs=placed, out_specs=P("row", "col", None), check_vma=False
    )
```

profile of v0, /device:TPU:0, one launch (start us, length us, event | category | flops | bytes accessed | tf_op | source)
XLA Modules:
  0.0 276.2 jit_solution(16021958013082864905)
XLA Ops:
  6.5 0.8 fusion.48
  7.4 6.2 %all-gather = bf16[4,48,32]{1,2,0:T(8,128)(2,1)S(1)} all-gather(bf16[1,48,32]{1,2,0:T(8,128)(2,1)S(1)} %bitcast.93), channel_id=1, replica_groups=mesh['row'=8,'col'=4] {'col'}, dimensions={0}, use_global_device_ids=true | all-gather | bytes 15360 | tf_op jit(solution)/shard_map/all_gather | solution.py:50
  13.6 0.1 reshape.97
  13.7 0.1 copy.69
  13.8 0.7 reshape.110
  14.5 6.2 %all-to-all-start.1 = ((bf16[8,2,384]{2,1,0:T(2,128)(2,1)}), bf16[8,2,384]{2,1,0:T(2,128)(2,1)S(1)}, u32[]{:S(2)}, u32[]{:S(2)}) async-start(bf16[8,2,384]{2,1,0:T(2,128)(2,1)} %reshape.110), calls=%async_computation.1 | async-start | bytes 24576 | tf_op jit(solution)/shard_map/all_to_all | solution.py:54
  20.8 1.4 convert_reduce_fusion
  22.2 0.5 fusion.2
  22.7 0.7 fusion.16
  23.4 0.6 copy.51
  24.1 13.4 %all_gather.18 = bf16[32,192,32]{2,0,1:T(8,128)(2,1)} all-gather(bf16[32,48,32]{2,0,1:T(8,128)(2,1)S(1)} %copy.51), channel_id=1, replica_groups=mesh['row'=8,'col'=4] {'col'}, dimensions={1}, use_global_device_ids=true | all-gather | bytes 491520 | tf_op jit(solution)/shard_map/all_gather | solution.py:49
  37.4 0.7 fusion.17
  38.1 45.3 %all_gather.19 = bf16[256,48,32]{1,2,0:T(8,128)(2,1)S(1)} all-gather(bf16[32,48,32]{1,2,0:T(8,128)(2,1)S(1)} %fusion.17), channel_id=1, replica_groups=mesh['row'=8,'col'=4] {'row'}, dimensions={0}, use_global_device_ids=true | all-gather | bytes 884736 | tf_op jit(solution)/shard_map/all_gather | solution.py:45
  83.6 3.8 %reshape.108 = bf16[8,2,12288]{2,1,0:T(2,128)(2,1)} reshape(bf16[192,32,32]{2,1,0:T(8,128)(2,1)} %bitcast.89) | data formatting | bytes 786432
  87.4 2.4 copy.56
  89.8 3.6 %all-to-all-start = ((bf16[8,2,12288]{2,1,0:T(2,128)(2,1)}), bf16[8,2,12288]{2,1,0:T(2,128)(2,1)S(1)}, u32[]{:S(2)}, u32[]{:S(2)}) async-start(bf16[8,2,12288]{2,1,0:T(2,128)(2,1)} %reshape.108), calls=%async_computation | async-start | bytes 786432 | tf_op jit(solution)/shard_map/all_to_all | solution.py:53
  93.4 35.2 %all_gather.21 = bf16[256,48]{1,0:T(8,128)(2,1)S(1)} all-gather(bf16[32,48]{1,0:T(8,128)(2,1)S(1)} %get-tuple-element.7), channel_id=1, replica_groups=mesh['row'=8,'col'=4] {'row'}, dimensions={0}, use_global_device_ids=true | all-gather | bytes 27648 | tf_op jit(solution)/shard_map/all_gather | solution.py:46
  128.7 0.1 reshape.111
  128.8 0.1 all_to_all.44
  128.9 0.1 convolution_maximum_fusion
  129.0 0.8 reshape.109
  129.8 0.6 copy.53
  130.4 1.0 reshape.93
  131.4 0.2 copy.54
  131.6 3.7 %convert_bitcast_fusion = bf16[24,48,32,32]{1,2,3,0:T(8,128)(2,1)} fusion(bf16[24,32,256,1]{2,1,3,0:T(8,128)(2,1)S(1)} %bitcast.90, bf16[48,32,256]{2,0,1:T(8,128)(2,1)S(1)} %copy-done.4), kind=kOutput, calls=%fused_computation | convolution fusion | flops 605159424 | bytes 3538944 | tf_op jit(solution)/shard_map/dot_general | solution.py:58
  135.3 17.8 %copy.57 = bf16[24,48,32,32]{3,2,1,0:T(8,128)(2,1)} copy(bf16[24,48,32,32]{1,2,3,0:T(8,128)(2,1)} %convert_bitcast_fusion) | data formatting | bytes 4718592 | tf_op jit(solution)/shard_map/convert_element_type | solution.py:67
  153.1 12.7 %reshape.95 = bf16[24,48,1024]{2,1,0:T(8,128)(2,1)S(1)} reshape(bf16[24,48,32,32]{3,2,1,0:T(8,128)(2,1)} %copy.57) | data formatting | bytes 4718592 | tf_op jit(solution)/shard_map/reshape | solution.py:69
  165.9 1.8 fusion.49
  167.8 0.4 multiply_reduce_fusion.2
  168.2 0.5 fusion.41
  168.7 1.2 fusion.22
  170.0 0.7 all-gather.6.cloned.1.call-update
  170.7 48.0 %all-gather.4.cloned.1.call-done = bf16[192,48,128]{2,1,0:T(8,128)(2,1)} async-done(((bf16[24,48,128]{2,1,0:T(8,128)(2,1)}), bf16[192,48,128]{2,1,0:T(8,128)(2,1)}) %all-gather.4.cloned.1.call-update) | async-done | bytes 2359312 | tf_op jit(solution)/shard_map/all_gather | solution.py:92
  218.7 3.9 %all-to-all-start.2 = ((bf16[192,48,128]{2,1,0:T(8,128)(2,1)}), bf16[192,48,128]{2,1,0:T(8,128)(2,1)S(1)}, u32[]{:S(2)}, u32[]{:S(2)}) async-start(bf16[192,48,128]{2,1,0:T(8,128)(2,1)} %all-gather.4.cloned.1.call-done), calls=%async_computation.2 | async-start | bytes 4718592 | tf_op jit(solution)/shard_map/all_to_all | solution.py:93
  222.6 1.3 fusion.9
  223.9 18.8 %all-gather.6.cloned.1.call-done = bf16[24,192,128]{2,1,0:T(8,128)(2,1)} async-done(((bf16[24,48,128]{2,1,0:T(8,128)(2,1)}), bf16[24,192,128]{2,1,0:T(8,128)(2,1)}) %all-gather.6.cloned.1.call-update) | async-done | bytes 1179664 | tf_op jit(solution)/shard_map/all_gather | solution.py:96
  242.7 2.8 %copy.63 = bf16[24,192,128]{1,0,2:T(8,128)(2,1)} copy(bf16[24,192,128]{2,1,0:T(8,128)(2,1)} %all-gather.6.cloned.1.call-done) | data formatting | bytes 2359296 | tf_op jit(solution)/shard_map/all_gather | solution.py:96
  245.5 11.6 %all-to-all-done.2 = bf16[192,48,128]{2,1,0:T(8,128)(2,1)S(1)} async-done(((bf16[192,48,128]{2,1,0:T(8,128)(2,1)}), bf16[192,48,128]{2,1,0:T(8,128)(2,1)S(1)}, u32[]{:S(2)}, u32[]{:S(2)}) %all-to-all-start.2) | async-done | bytes 2359328 | tf_op jit(solution)/shard_map/all_to_all | solution.py:93
  257.1 2.1 copy.61
  259.2 3.8 %copy.62 = bf16[48,192,128]{1,0,2:T(8,128)(2,1)S(1)} copy(bf16[48,192,128]{2,1,0:T(8,128)(2,1)} %bitcast.86) | data formatting | bytes 4718592 | tf_op jit(solution)/shard_map/all_to_all | solution.py:93
  263.0 2.4 bitcast_reduce_fusion
  265.4 0.3 multiply_reduce_fusion
  265.7 0.2 multiply_convert_fusion
  265.9 0.8 copy-done.2
  266.7 0.2 copy-done.5
  266.9 0.5 fusion.50
  267.4 0.4 multiply_reduce_fusion.1
  267.8 1.5 fusion.15
  (45 shorter events, 0.5 us)
Async XLA Ops:
  6.5 159.3 %copy-start = (bf16[1024,128]{1,0:T(8,128)(2,1)S(1)}, bf16[1024,128]{1,0:T(8,128)(2,1)}, u32[]{:S(2)}) copy-start(bf16[1024,128]{1,0:T(8,128)(2,1)} %param.18) | copy-start | bytes 786436
  6.5 15.7 %copy-start.3 = (bf16[32,48,256]{2,1,0:T(8,128)(2,1)S(1)}, bf16[32,48,256]{2,1,0:T(8,128)(2,1)}, u32[]{:S(2)}) copy-start(bf16[32,48,256]{2,1,0:T(8,128)(2,1)} %param.12) | copy-start | bytes 2359300
  6.5 16.2 %copy-start.11 = (bf16[256,32]{0,1:T(8,128)(2,1)S(1)}, bf16[256,32]{0,1:T(8,128)(2,1)}, u32[]{:S(2)}) copy-start(bf16[256,32]{0,1:T(8,128)(2,1)} %param.16) | copy-start | bytes 49156
  14.5 75.3 %all-to-all-start.1 = ((bf16[8,2,384]{2,1,0:T(2,128)(2,1)}), bf16[8,2,384]{2,1,0:T(2,128)(2,1)S(1)}, u32[]{:S(2)}, u32[]{:S(2)}) async-start(bf16[8,2,384]{2,1,0:T(2,128)(2,1)} %reshape.110), calls=%async_computation.1 | async-start | bytes 24576 | tf_op jit(solution)/shard_map/all_to_all | solution.py:54
  23.4 14.0 %copy-start.12 = (bf16[256,32]{0,1:T(8,128)(2,1)S(1)}, bf16[256,32]{0,1:T(8,128)(2,1)}, u32[]{:S(2)}) copy-start(bf16[256,32]{0,1:T(8,128)(2,1)} %param.17) | copy-start | bytes 49156
  38.1 45.4 %copy-start.13 = (s32[192]{0:T(256)S(1)}, s32[192]{0:T(256)}, u32[]{:S(2)}) copy-start(s32[192]{0:T(256)} %param.14) | copy-start | bytes 2308
  89.8 39.2 %all-to-all-start = ((bf16[8,2,12288]{2,1,0:T(2,128)(2,1)}), bf16[8,2,12288]{2,1,0:T(2,128)(2,1)S(1)}, u32[]{:S(2)}, u32[]{:S(2)}) async-start(bf16[8,2,12288]{2,1,0:T(2,128)(2,1)} %reshape.108), calls=%async_computation | async-start | bytes 786432 | tf_op jit(solution)/shard_map/all_to_all | solution.py:53
  93.4 125.3 %all-gather.4.cloned.1.call-start = ((), (), s32[]{:S(2)}) async-start(), calls=%async_computation.3 | async-start | bytes 2654208 | tf_op jit(solution)/shard_map/all_gather | solution.py:92
  130.4 1.2 copy-start.4
  165.9 2.3 copy-start.6
  167.7 54.8 %copy-start.1 = (f32[24,48,128]{2,1,0:T(8,128)}, f32[24,48,128]{2,1,0:T(8,128)S(1)}, u32[]{:S(2)}) copy-start(f32[24,48,128]{2,1,0:T(8,128)S(1)} %get-tuple-element.10) | copy-start | bytes 1769476
  169.9 72.8 %all-gather.6.cloned.1.call-start = ((), (), s32[]{:S(2)}) async-start(), calls=%async_computation.4 | async-start | bytes 1474560 | tf_op jit(solution)/shard_map/all_gather | solution.py:96
  170.7 51.9 %copy-start.10 = (bf16[128,128]{1,0:T(8,128)(2,1)S(1)}, bf16[128,128]{1,0:T(8,128)(2,1)}, u32[]{:S(2)}) copy-start(bf16[128,128]{1,0:T(8,128)(2,1)} %param.20) | copy-start | bytes 98308
  218.7 38.4 %all-to-all-start.2 = ((bf16[192,48,128]{2,1,0:T(8,128)(2,1)}), bf16[192,48,128]{2,1,0:T(8,128)(2,1)S(1)}, u32[]{:S(2)}, u32[]{:S(2)}) async-start(bf16[192,48,128]{2,1,0:T(8,128)(2,1)} %all-gather.4.cloned.1.call-done), calls=%async_computation.2 | async-start | bytes 4718592 | tf_op jit(solution)/shard_map/all_to_all | solution.py:93
  265.6 1.1 copy-start.2
  265.6 1.2 copy-start.5
  265.6 1.2 copy-start.7
  266.9 0.9 copy-start.8
  266.9 1.0 copy-start.9
Sparse Core Ops, SparseCore 0:
  170.0 48.6 all-gather.3
  220.2 22.3 all-gather.5
where the time goes:
time: 277 us; the launch traced here: 276 us
  blocking collectives  100 us (36%)
  waiting for transfers between devices  79.1 us (29%)
  local copies, waits for them, and re-layouts  50.8 us (18%)
  starting transfers between devices  13.7 us (5%)
  between operations  13.7 us (5%)
  matrix products  13.2 us (5%)
  other arithmetic  5.45 us (2%)
    all_gather x1, waiting for transfers between devices, shards(): right_cols = lax.all_gather(right_tri, 'row', axis=0, tiled=True)  48 us
    all_gather x1, blocking collectives, shards(): lax.all_gather(right_side, 'row', axis=0, tiled=True)  45.3 us
    all_gather x1, blocking collectives, shards(): lax.all_gather(mask_wire, 'row', axis=0, tiled=True)  35.2 us
    all_gather x1, waiting for transfers between devices, shards(): lax.all_gather(left_tri, 'col', axis=1, tiled=True)  18.8 us
    convert_element_type x1, local copies, waits for them, and re-layouts, shards(): outer = outer.reshape(block_rows, narrow, block_cols, narrow).transpose(0...  17.8 us
    all_gather x1, blocking collectives, shards(): lax.all_gather(left_side, 'col', axis=1, tiled=True)  13.4 us
    reshape x1, local copies, waits for them, and re-layouts, shards(): outer = outer.reshape(block_rows, block_cols, narrow * narrow)  12.7 us
    all_to_all x1, waiting for transfers between devices, shards(): lax.all_to_all(right_cols, 'col', split_axis=0, concat_axis=1, tiled=True)  11.6 us
  transfers between devices with their start and end apart: 5, of which 3 were waited for; matrix products, arithmetic and copies ran while one was open for 5% of the time, Pallas kernels for 0%

commit v1 on v0

--- a/solution.py
+++ b/solution.py
@@ -4,6 +4,18 @@
 from jax.sharding import PartitionSpec as P
 
 epsilon = 1e-05
+
+
+def ring_product(x, axis, dim, contribution):
+    peers, index = (lax.axis_size(axis), lax.axis_index(axis))
+    downward = [(i, (i - 1) % peers) for i in range(peers)]
+    extent = x.shape[dim]
+    held = x
+    total = contribution(held, index * extent)
+    for step in range(1, peers):
+        held = lax.ppermute(held, axis, downward)
+        total = total + contribution(held, (index + step) % peers * extent)
+    return total
 
 
 def normalize(values):
@@ -91,11 +103,16 @@
     ).astype(jnp.bfloat16)
     right_cols = lax.all_gather(right_tri, "row", axis=0, tiled=True)
     right_rows = lax.all_to_all(right_cols, "col", split_axis=0, concat_axis=1, tiled=True)
-    summed = jnp.einsum(
-        "ikc,jkc->ijc",
-        lax.all_gather(left_tri, "col", axis=1, tiled=True),
-        right_rows,
-        preferred_element_type=jnp.float32,
+    summed = ring_product(
+        left_tri,
+        "col",
+        1,
+        lambda part, offset: jnp.einsum(
+            "ikc,jkc->ijc",
+            part,
+            lax.dynamic_slice_in_dim(right_rows, offset, part.shape[1], axis=1),
+            preferred_element_type=jnp.float32,
+        ),
     )
     normed_sum = normalize(summed).astype(jnp.bfloat16)
     update = jax.nn.sigmoid(

time: 277 us -> 296 us (1.069)
  local copies, waits for them, and re-layouts: 50.8 us -> 58.5 us
  starting transfers between devices: 13.7 us -> 19.1 us
  matrix products: 13.2 us -> 17.2 us
    ppermute x0 -> x3, waiting for transfers between devices: none -> 32 us  [ring_product(): held = lax.ppermute(held, axis, downward)]
    all_gather x1 -> x0, waiting for transfers between devices: 18.8 us -> none  [shards(): lax.all_gather(left_tri, 'col', axis=1, tiled=True)]
    all_to_all x1, waiting for transfers between devices: 11.6 us -> 0.01 us  [shards(): lax.all_to_all(right_cols, 'col', split_axis=0, concat_axis=1, tiled=True)]
    unnamed x33 -> x47, local copies, waits for them, and re-layouts: 6.54 us -> 13.9 us
    ppermute x0 -> x3, local copies, waits for them, and re-layouts: none -> 5.66 us  [ring_product(): held = lax.ppermute(held, axis, downward)]
    ppermute x0 -> x3, starting transfers between devices: none -> 5.63 us  [ring_product(): held = lax.ppermute(held, axis, downward)]
    all_to_all x2 -> x1, local copies, waits for them, and re-layouts: 5.89 us -> 0.71 us  [shards(): lax.all_to_all(right_cols, 'col', split_axis=0, concat_axis=1, tiled=True)]
    dot_general x1 -> x4, matrix products: 2.35 us -> 5.48 us  [shards(): jnp.einsum('ikc,jkc->ijc', part, lax.dynamic_slice_in_dim(right_rows, off...]
  transfers between devices with their start and end apart: 5 -> 7, of which waited for: 3 -> 3; matrix products, arithmetic and copies ran while one was open for 5% -> 7% of each run, Pallas kernels for 0% -> 0%
where the time goes in v1:
time: 296 us; the launch traced here: 295 us
  blocking collectives  100 us (34%)
  waiting for transfers between devices  80.8 us (27%)
  local copies, waits for them, and re-layouts  58.5 us (20%)
  starting transfers between devices  19.1 us (6%)
  matrix products  17.2 us (6%)
  between operations  13.8 us (5%)
  other arithmetic  5.36 us (2%)
    all_gather x1, waiting for transfers between devices, shards(): right_cols = lax.all_gather(right_tri, 'row', axis=0, tiled=True)  48.8 us
    all_gather x1, blocking collectives, shards(): lax.all_gather(right_side, 'row', axis=0, tiled=True)  45.3 us
    all_gather x1, blocking collectives, shards(): lax.all_gather(mask_wire, 'row', axis=0, tiled=True)  35.2 us
    ppermute x3, waiting for transfers between devices, ring_product(): held = lax.ppermute(held, axis, downward)  32 us
    convert_element_type x1, local copies, waits for them, and re-layouts, shards(): outer = outer.reshape(block_rows, narrow, block_cols, narrow).transpose(0...  17.8 us
    unnamed x47, local copies, waits for them, and re-layouts  13.9 us
    all_gather x1, blocking collectives, shards(): lax.all_gather(left_side, 'col', axis=1, tiled=True)  13.4 us
    reshape x1, local copies, waits for them, and re-layouts, shards(): outer = outer.reshape(block_rows, block_cols, narrow * narrow)  12.7 us
  transfers between devices with their start and end apart: 7, of which 3 were waited for; matrix products, arithmetic and copies ran while one was open for 7% of the time, Pallas kernels for 0%

profile of v1, /device:TPU:0, one launch (start us, length us, event | category | flops | bytes accessed | tf_op | source)
XLA Modules:
  0.0 294.9 jit_solution(18066530004756536214)
XLA Ops:
  6.5 0.8 fusion.48
  7.4 6.2 %all-gather = bf16[4,48,32]{1,2,0:T(8,128)(2,1)S(1)} all-gather(bf16[1,48,32]{1,2,0:T(8,128)(2,1)S(1)} %bitcast.99), channel_id=1, replica_groups=mesh['row'=8,'col'=4] {'col'}, dimensions={0}, use_global_device_ids=true | all-gather | bytes 15360 | tf_op jit(solution)/shard_map/all_gather | solution.py:62
  13.8 0.7 reshape.110
  14.5 6.2 %all-to-all-start.1 = ((bf16[8,2,384]{2,1,0:T(2,128)(2,1)}), bf16[8,2,384]{2,1,0:T(2,128)(2,1)S(1)}, u32[]{:S(2)}, u32[]{:S(2)}) async-start(bf16[8,2,384]{2,1,0:T(2,128)(2,1)} %reshape.110), calls=%async_computation.1 | async-start | bytes 24576 | tf_op jit(solution)/shard_map/all_to_all | solution.py:66
  20.8 1.4 convert_reduce_fusion
  22.7 0.7 fusion.16
  23.4 0.6 copy.72
  24.1 13.4 %all_gather.15 = bf16[32,192,32]{2,0,1:T(8,128)(2,1)} all-gather(bf16[32,48,32]{2,0,1:T(8,128)(2,1)S(1)} %copy.72), channel_id=1, replica_groups=mesh['row'=8,'col'=4] {'col'}, dimensions={1}, use_global_device_ids=true | all-gather | bytes 491520 | tf_op jit(solution)/shard_map/all_gather | solution.py:61
  37.4 0.7 fusion.17
  38.1 45.3 %all_gather.16 = bf16[256,48,32]{1,2,0:T(8,128)(2,1)S(1)} all-gather(bf16[32,48,32]{1,2,0:T(8,128)(2,1)S(1)} %fusion.17), channel_id=1, replica_groups=mesh['row'=8,'col'=4] {'row'}, dimensions={0}, use_global_device_ids=true | all-gather | bytes 884736 | tf_op jit(solution)/shard_map/all_gather | solution.py:57
  83.6 3.8 %reshape.108 = bf16[8,2,12288]{2,1,0:T(2,128)(2,1)} reshape(bf16[192,32,32]{2,1,0:T(8,128)(2,1)} %bitcast.95) | data formatting | bytes 786432
  87.4 2.4 copy.77
  89.8 3.6 %all-to-all-start = ((bf16[8,2,12288]{2,1,0:T(2,128)(2,1)}), bf16[8,2,12288]{2,1,0:T(2,128)(2,1)S(1)}, u32[]{:S(2)}, u32[]{:S(2)}) async-start(bf16[8,2,12288]{2,1,0:T(2,128)(2,1)} %reshape.108), calls=%async_computation | async-start | bytes 786432 | tf_op jit(solution)/shard_map/all_to_all | solution.py:65
  93.4 35.2 %all_gather.18 = bf16[256,48]{1,0:T(8,128)(2,1)S(1)} all-gather(bf16[32,48]{1,0:T(8,128)(2,1)S(1)} %get-tuple-element.11), channel_id=1, replica_groups=mesh['row'=8,'col'=4] {'row'}, dimensions={0}, use_global_device_ids=true | all-gather | bytes 27648 | tf_op jit(solution)/shard_map/all_gather | solution.py:58
  129.0 0.8 reshape.109
  129.8 0.6 copy.74
  130.4 1.0 reshape.93
  131.6 3.7 %convert_bitcast_fusion = bf16[24,48,32,32]{1,2,3,0:T(8,128)(2,1)} fusion(bf16[24,32,256,1]{2,1,3,0:T(8,128)(2,1)S(1)} %bitcast.96, bf16[48,32,256]{2,0,1:T(8,128)(2,1)S(1)} %copy-done.5), kind=kOutput, calls=%fused_computation | convolution fusion | flops 605159424 | bytes 3538944 | tf_op jit(solution)/shard_map/dot_general | solution.py:70
  135.4 17.8 %copy.78 = bf16[24,48,32,32]{3,2,1,0:T(8,128)(2,1)} copy(bf16[24,48,32,32]{1,2,3,0:T(8,128)(2,1)} %convert_bitcast_fusion) | data formatting | bytes 4718592 | tf_op jit(solution)/shard_map/convert_element_type | solution.py:79
  153.2 12.7 %reshape.95 = bf16[24,48,1024]{2,1,0:T(8,128)(2,1)S(1)} reshape(bf16[24,48,32,32]{3,2,1,0:T(8,128)(2,1)} %copy.78) | data formatting | bytes 4718592 | tf_op jit(solution)/shard_map/reshape | solution.py:81
  165.9 1.8 fusion.49
  168.3 0.5 fusion.41
  168.8 1.1 fusion.22
  169.9 48.8 %all-gather.3.cloned.1.call-done = bf16[192,48,128]{2,1,0:T(8,128)(2,1)} async-done(((bf16[24,48,128]{2,1,0:T(8,128)(2,1)}), bf16[192,48,128]{2,1,0:T(8,128)(2,1)}) %all-gather.3.cloned.1.call-update) | async-done | bytes 2359312 | tf_op jit(solution)/shard_map/all_gather | solution.py:104
  218.6 3.6 %all-to-all-start.2 = ((bf16[192,48,128]{2,1,0:T(8,128)(2,1)}), bf16[192,48,128]{2,1,0:T(8,128)(2,1)S(1)}, u32[]{:S(2)}, u32[]{:S(2)}) async-start(bf16[192,48,128]{2,1,0:T(8,128)(2,1)} %all-gather.3.cloned.1.call-done), calls=%async_computation.2 | async-start | bytes 4718592 | tf_op jit(solution)/shard_map/all_to_all | solution.py:105
  222.3 1.7 collective-permute-start
  224.0 27.8 %collective-permute-done = bf16[24,48,128]{2,1,0:T(8,128)(2,1)S(1)} collective-permute-done((bf16[24,48,128]{2,1,0:T(8,128)(2,1)S(1)}, bf16[24,48,128]{2,1,0:T(8,128)(2,1)S(1)}, u32[]{:S(2)}, u32[]{:S(2)}) %collective-permute-start) | collective-permute-done | bytes 294944 | tf_op jit(solution)/shard_map/ppermute | solution.py:16
  251.8 0.7 copy-done.10
  252.5 1.9 collective-permute-start.1
  254.4 4.2 %collective-permute-done.1 = bf16[24,48,128]{2,1,0:T(8,128)(2,1)} collective-permute-done((bf16[24,48,128]{2,1,0:T(8,128)(2,1)S(1)}, bf16[24,48,128]{2,1,0:T(8,128)(2,1)}, u32[]{:S(2)}, u32[]{:S(2)}) %collective-permute-start.1) | collective-permute-done | bytes 294944 | tf_op jit(solution)/shard_map/ppermute | solution.py:16
  258.7 2.0 collective-permute-start.2
  260.7 1.3 copy.84
  262.0 2.1 fusion.9
  264.1 1.2 copy.86
  265.3 2.2 copy.88
  267.5 2.2 copy.90
  269.7 0.7 copy.82
  270.5 1.4 constant_dynamic-slice_fusion
  271.8 1.7 copy.98
  273.5 1.7 copy.97
  275.2 1.0 copy.99
  276.2 1.8 copy.100
  278.0 2.7 fusion.52
  280.8 0.9 fusion.51
  281.9 0.9 fusion.53
  283.0 1.0 bitcast_reduce_fusion
  284.5 0.8 copy-done.3
  286.5 1.5 fusion.15
  (68 shorter events, 4.0 us)
Async XLA Ops:
  6.5 159.4 %copy-start = (bf16[1024,128]{1,0:T(8,128)(2,1)S(1)}, bf16[1024,128]{1,0:T(8,128)(2,1)}, u32[]{:S(2)}) copy-start(bf16[1024,128]{1,0:T(8,128)(2,1)} %param.18) | copy-start | bytes 786436
  6.5 15.7 %copy-start.4 = (bf16[32,48,256]{2,1,0:T(8,128)(2,1)S(1)}, bf16[32,48,256]{2,1,0:T(8,128)(2,1)}, u32[]{:S(2)}) copy-start(bf16[32,48,256]{2,1,0:T(8,128)(2,1)} %param.12) | copy-start | bytes 2359300
  6.5 16.2 %copy-start.16 = (bf16[256,32]{0,1:T(8,128)(2,1)S(1)}, bf16[256,32]{0,1:T(8,128)(2,1)}, u32[]{:S(2)}) copy-start(bf16[256,32]{0,1:T(8,128)(2,1)} %param.16) | copy-start | bytes 49156
  14.5 75.3 %all-to-all-start.1 = ((bf16[8,2,384]{2,1,0:T(2,128)(2,1)}), bf16[8,2,384]{2,1,0:T(2,128)(2,1)S(1)}, u32[]{:S(2)}, u32[]{:S(2)}) async-start(bf16[8,2,384]{2,1,0:T(2,128)(2,1)} %reshape.110), calls=%async_computation.1 | async-start | bytes 24576 | tf_op jit(solution)/shard_map/all_to_all | solution.py:66
  23.4 14.0 %copy-start.17 = (bf16[256,32]{0,1:T(8,128)(2,1)S(1)}, bf16[256,32]{0,1:T(8,128)(2,1)}, u32[]{:S(2)}) copy-start(bf16[256,32]{0,1:T(8,128)(2,1)} %param.17) | copy-start | bytes 49156
  38.1 45.4 %copy-start.18 = (s32[192]{0:T(256)S(1)}, s32[192]{0:T(256)}, u32[]{:S(2)}) copy-start(s32[192]{0:T(256)} %param.14) | copy-start | bytes 2308
  89.8 39.2 %all-to-all-start = ((bf16[8,2,12288]{2,1,0:T(2,128)(2,1)}), bf16[8,2,12288]{2,1,0:T(2,128)(2,1)S(1)}, u32[]{:S(2)}, u32[]{:S(2)}) async-start(bf16[8,2,12288]{2,1,0:T(2,128)(2,1)} %reshape.108), calls=%async_computation | async-start | bytes 786432 | tf_op jit(solution)/shard_map/all_to_all | solution.py:65
  93.4 125.3 %all-gather.3.cloned.1.call-start = ((), (), s32[]{:S(2)}) async-start(), calls=%async_computation.3 | async-start | bytes 2654208 | tf_op jit(solution)/shard_map/all_gather | solution.py:104
  130.4 1.2 copy-start.5
  165.9 2.3 copy-start.12
  167.8 94.2 %copy-start.2 = (f32[24,48,128]{2,1,0:T(8,128)}, f32[24,48,128]{2,1,0:T(8,128)S(1)}, u32[]{:S(2)}) copy-start(f32[24,48,128]{2,1,0:T(8,128)S(1)} %get-tuple-element.14) | copy-start | bytes 1769476
  218.6 51.1 %all-to-all-start.2 = ((bf16[192,48,128]{2,1,0:T(8,128)(2,1)}), bf16[192,48,128]{2,1,0:T(8,128)(2,1)S(1)}, u32[]{:S(2)}, u32[]{:S(2)}) async-start(bf16[192,48,128]{2,1,0:T(8,128)(2,1)} %all-gather.3.cloned.1.call-done), calls=%async_computation.2 | async-start | bytes 4718592 | tf_op jit(solution)/shard_map/all_to_all | solution.py:105
  222.3 29.5 %collective-permute-start = (bf16[24,48,128]{2,1,0:T(8,128)(2,1)S(1)}, bf16[24,48,128]{2,1,0:T(8,128)(2,1)S(1)}, u32[]{:S(2)}, u32[]{:S(2)}) collective-permute-start(bf16[24,48,128]{2,1,0:T(8,128)(2,1)S(1)} %get-tuple-element.5), channel_id=1, source_target_pairs={{0,3},{1,0},{2,1},{3,2},{4,7},{5,4},{6,5},{7,6},{8,11},{9,8},{10,9... | collective-permute-start | bytes 884744 | tf_op jit(solution)/shard_map/ppermute | solution.py:16
  251.8 0.7 copy-start.10
  252.5 6.1 %collective-permute-start.1 = (bf16[24,48,128]{2,1,0:T(8,128)(2,1)S(1)}, bf16[24,48,128]{2,1,0:T(8,128)(2,1)}, u32[]{:S(2)}, u32[]{:S(2)}) collective-permute-start(bf16[24,48,128]{2,1,0:T(8,128)(2,1)S(1)} %collective-permute-done), channel_id=1, source_target_pairs={{0,3},{1,0},{2,1},{3,2},{4,7},{5,4},{6,5},{7,6},{8,11},{9,8},{10,9... | collective-permute-start | bytes 884744 | tf_op jit(solution)/shard_map/ppermute | solution.py:16
  258.7 8.9 %collective-permute-start.2 = (bf16[24,48,128]{2,1,0:T(8,128)(2,1)}, bf16[24,48,128]{2,1,0:T(8,128)(2,1)}, u32[]{:S(2)}, u32[]{:S(2)}) collective-permute-start(bf16[24,48,128]{2,1,0:T(8,128)(2,1)} %collective-permute-done.1), channel_id=1, source_target_pairs={{0,3},{1,0},{2,1},{3,2},{4,7},{5,4},{6,5},{7,6},{8,11},{9,8},{10,9... | collective-permute-start | bytes 884744 | tf_op jit(solution)/shard_map/ppermute | solution.py:16
  261.9 2.1 copy-start.11
  278.0 2.7 copy-start.1
  278.0 2.7 copy-start.7
  280.7 1.1 copy-start.8
  281.9 1.1 copy-start.6
  284.3 1.1 copy-start.3
  284.3 1.2 copy-start.9
  284.3 1.2 copy-start.13
  285.5 0.9 copy-start.14
  285.5 1.0 copy-start.15
Sparse Core Ops, SparseCore 0:
  170.0 48.6 all-gather.2
